TPU v7x, 512 devices: a whole 4x8x8 slice. The times are simulated.
512 devices in a mesh: occ: 64 (over x, y, core), aux: 8 (over z).
Axes of the slice: x: 4, y: 8, z: 8, core: 2. Of those that a mesh axis runs over, the one named last changes fastest.
Arguments:
- ao_blocks: bfloat16 [256, 256, 8192], P('occ', None, 'aux'), may hold values from -0.59765625 to 0.59765625
- pno_coef: bfloat16 [1024, 256, 200], P('occ'), may hold values from -0.375 to 0.375
- pno_energy: float32 [1024, 200], P('occ'), may hold values from 0.3 to 3
- occ_energy: float32 [256], replicated, may hold values from -1.5 to -0.3
- pair_partner: int32 [1024], P('occ'), may hold values from 0 to 255, as said below
- pno_count: int32 [1024], P('occ'), may hold values from 40 to 200, as said below
Outputs:
- amplitudes: float32 [1024, 200, 200], P(('occ', 'aux'))
- orbital_pair_energy: float32 [256], P('occ')
Inputs may be any that keep to these rules, and one draw needn't show every extreme that they name: pair_partner[s] differs from own(s) and is an orbital owned by the same index of occ as own(s), or by the index just below or just above it. `pno_count`: every count is a multiple of 8; in every block of 16 pairs one count is 200 and one is 40.
All inputs are finite; a program needn't handle non-finite values.
Results may differ from a plain program's by a relative error of at most 0.0041.
Values may be sent and summed in bfloat16 or wider, within the bound.
A program may use at most 128 MiB of HBM per device.

v0:
```python
import jax
import jax.numpy as jnp
from jax import lax
from jax.sharding import PartitionSpec as P


def padded(cells, sides, width):
    for axis, dim in sides:
        count = lax.axis_size(axis)
        ends = count - 1
        head = lax.slice_in_dim(cells, 0, width, axis=dim)
        tail = lax.slice_in_dim(cells, cells.shape[dim] - width, cells.shape[dim], axis=dim)
        cells = jnp.concatenate(
            [
                lax.ppermute(tail, axis, [(i, (i + 1) % count) for i in range(ends)]),
                cells,
                lax.ppermute(head, axis, [((i + 1) % count, i) for i in range(ends)]),
            ],
            axis=dim,
        )
    return cells


def shards(ao_blocks, pno_coef, pno_energy, occ_energy, pair_partner, pno_count):
    orb_dev = ao_blocks.shape[0]
    virtuals = ao_blocks.shape[1]
    aux_block = ao_blocks.shape[2]
    pair_dev = pno_coef.shape[0]
    pno_max = pno_coef.shape[2]
    per_orbital = pair_dev // orb_dev
    occ_place = lax.axis_index("occ")
    aux_place = lax.axis_index("aux")
    columns = jnp.arange(pno_max, dtype=jnp.int32)
    kept_mask = (columns[None, :] < pno_count[:, None]).astype(jnp.bfloat16)
    masked_coef = pno_coef * kept_mask[:, None, :]
    projected_own = (
        jnp.einsum(
            "ornp,onk->orpk",
            masked_coef.reshape(orb_dev, per_orbital, virtuals, pno_max),
            ao_blocks,
            preferred_element_type=jnp.float32,
        )
        .astype(jnp.bfloat16)
        .reshape(pair_dev, pno_max, aux_block)
    )
    nearby = padded(ao_blocks, (("occ", 0),), orb_dev)
    window_slot = pair_partner - (occ_place - 1) * orb_dev
    partner_blocks = jnp.take(nearby, window_slot, axis=0)
    projected_partner = jnp.einsum(
        "snp,snk->spk", masked_coef, partner_blocks, preferred_element_type=jnp.float32
    ).astype(jnp.bfloat16)
    partials = jnp.einsum(
        "spk,sqk->spq", projected_own, projected_partner, preferred_element_type=jnp.float32
    )
    share_rows = pair_dev // lax.axis_size("aux")
    first_row = aux_place * share_rows
    totals = lax.psum(partials, "aux")
    exchange_ints = lax.dynamic_slice_in_dim(totals, first_row, share_rows, 0)
    own_orbital = occ_place * orb_dev + jnp.arange(pair_dev, dtype=jnp.int32) // per_orbital
    mine_owner = lax.dynamic_slice_in_dim(own_orbital, first_row, share_rows, 0)
    mine_partner = lax.dynamic_slice_in_dim(pair_partner, first_row, share_rows, 0)
    energies = lax.dynamic_slice_in_dim(pno_energy, first_row, share_rows, 0)
    shift_occ = occ_energy[mine_owner] + occ_energy[mine_partner]
    denominator = energies[:, :, None] + energies[:, None, :] - shift_occ[:, None, None]
    amplitudes = -exchange_ints / denominator
    pair_energy = jnp.sum(
        (2.0 * exchange_ints - jnp.swapaxes(exchange_ints, 1, 2)) * amplitudes, axis=(1, 2)
    )
    half_energy = 0.5 * pair_energy
    orbital_ids = jnp.arange(occ_energy.shape[0], dtype=jnp.int32)
    hits = (orbital_ids[None, :] == mine_owner[:, None]).astype(jnp.float32) + (
        orbital_ids[None, :] == mine_partner[:, None]
    ).astype(jnp.float32)
    spread = jnp.sum(hits * half_energy[:, None], axis=0)
    whole_sum = lax.psum(spread, ("occ", "aux"))
    orbital = lax.dynamic_slice_in_dim(whole_sum, occ_place * orb_dev, orb_dev, 0)
    return (amplitudes, orbital)


def solution(mesh):
    return jax.shard_map(
        shards,
        mesh=mesh,
        in_specs=(
            P("occ", None, "aux"),
            P("occ", None, None),
            P("occ", None),
            P(),
            P("occ"),
            P("occ"),
        ),
        out_specs=(P(("occ", "aux"), None, None), P("occ")),
        check_vma=False,
    )
```

profile of v0, /device:TPU:1, one launch (start us, length us, event | category | flops | bytes accessed | tf_op | source)
XLA Modules:
  0.0 275.3 jit_solution(15171100014383080903)
XLA Ops:
  7.2 0.0 copy-start
  7.2 0.0 copy-start.2
  7.2 0.0 all-reduce.2.cloned.1.call-start
  7.2 4.7 %collective-permute-start = (bf16[4,256,1024]{2,1,0:T(8,128)(2,1)}, bf16[4,256,1024]{2,1,0:T(8,128)(2,1)}, u32[]{:S(2)}, u32[]{:S(2)}) collective-permute-start(bf16[4,256,1024]{2,1,0:T(8,128)(2,1)} %param.6), channel_id=1, source_target_pairs={{0,8},{8,16},{16,24},{24,32},{32,40},{40,48},{48,56},{56,64},{64,7... | collective-permute-start | bytes 6291464 | tf_op jit(solution)/shard_map/ppermute | solution.py:15
  12.0 6.8 %collective-permute-start.1 = (bf16[4,256,1024]{2,1,0:T(8,128)(2,1)}, bf16[4,256,1024]{2,1,0:T(8,128)(2,1)}, u32[]{:S(2)}, u32[]{:S(2)}) collective-permute-start(bf16[4,256,1024]{2,1,0:T(8,128)(2,1)} %param.6), channel_id=1, source_target_pairs={{8,0},{16,8},{24,16},{32,24},{40,32},{48,40},{56,48},{64,56},{72,6... | collective-permute-start | bytes 6291464 | tf_op jit(solution)/shard_map/ppermute | solution.py:17
  18.7 0.7 compare_and_fusion
  19.4 0.7 fusion.13
  20.1 1.9 broadcast_multiply_fusion
  22.0 0.0 copy-start.3
  22.1 0.0 copy-done.2
  22.1 4.7 %convolution_convert_fusion = bf16[4,4,200,1024]{3,2,1,0:T(8,128)(2,1)} fusion(bf16[4,4,256,200]{2,3,1,0:T(8,128)(2,1)S(1)} %bitcast.16, bf16[4,256,1024]{2,1,0:T(8,128)(2,1)S(1)} %copy-done.2), kind=kOutput, calls=%fused_computation.8 | convolution fusion | flops 1680998400 | bytes 10289152 | tf_op jit(solution)/shard_map/ornp,onk->orpk/dot_general | solution.py:37
  26.8 0.0 copy-done.3
  26.8 8.5 %collective-permute-done = bf16[4,256,1024]{2,1,0:T(8,128)(2,1)} collective-permute-done((bf16[4,256,1024]{2,1,0:T(8,128)(2,1)}, bf16[4,256,1024]{2,1,0:T(8,128)(2,1)}, u32[]{:S(2)}, u32[]{:S(2)}) %collective-permute-start) | collective-permute-done | bytes 2097184 | tf_op jit(solution)/shard_map/ppermute | solution.py:15
  35.2 4.4 %collective-permute-done.1 = bf16[4,256,1024]{2,1,0:T(8,128)(2,1)} collective-permute-done((bf16[4,256,1024]{2,1,0:T(8,128)(2,1)}, bf16[4,256,1024]{2,1,0:T(8,128)(2,1)}, u32[]{:S(2)}, u32[]{:S(2)}) %collective-permute-start.1) | collective-permute-done | bytes 2097184 | tf_op jit(solution)/shard_map/ppermute | solution.py:17
  39.6 5.5 %pad_maximum_fusion = bf16[12,256,1024]{2,1,0:T(8,128)(2,1)} fusion(bf16[4,256,1024]{2,1,0:T(8,128)(2,1)} %collective-permute-done.1, bf16[4,256,1024]{2,1,0:T(8,128)(2,1)S(1)} %copy-done.2, bf16[4,256,1024]{2,1,0:T(8,128)(2,1)} %collective-permute-done), kind=kLoop, calls=%fused_computation.7 | loop fusion | flops 6291456 | bytes 12582912 | tf_op jit(solution)/shard_map/concatenate | solution.py:13
  45.1 7.7 %gather_fusion = bf16[16,256,1024]{2,1,0:T(8,128)(2,1)} fusion(bf16[12,256,1024]{2,1,0:T(8,128)(2,1)} %pad_maximum_fusion, s32[1024]{0:T(1024)S(1)} %pad_clamp_fusion.2), kind=kCustom, calls=%fused_computation | custom fusion | bytes 16777280 | tf_op jit(solution)/shard_map/jit(_take)/gather | solution.py:48
  52.8 0.0 copy-done.4
  52.8 10.8 %fusion.9 = f32[16,200,200]{2,1,0:T(8,128)} fusion(bf16[16,200,1024]{2,1,0:T(8,128)(2,1)} %bitcast.17, bf16[16,256,200]{1,2,0:T(8,128)(2,1)S(1)} %copy-done.4, bf16[16,256,1024]{2,1,0:T(8,128)(2,1)} %gather_fusion, pred[16]{0:T(512)(128)(4,1)S(1)} %get-tuple-element.12), kind=kOutput, calls=%fused_computation.11 | convolution fusion | flops 2995912704 | bytes 19140624 | tf_op jit(solution)/shard_map/spk,sqk->spq/dot_general | solution.py:52
  63.6 0.0 all-reduce.2.cloned.1.call-update
  63.6 0.0 copy-done.5
  63.6 0.1 compare_select_fusion
  63.7 0.0 copy-done.1
  63.7 0.6 gather_fusion.1
  64.3 0.6 gather_fusion.2
  65.0 102.3 %all-reduce.2.cloned.1.call-done = f32[16,200,200]{2,1,0:T(8,128)} async-done(((f32[16,200,200]{2,1,0:T(8,128)}), f32[16,200,200]{2,1,0:T(8,128)}) %all-reduce.2.cloned.1.call-update) | async-done | bytes 2560016 | tf_op jit(solution)/shard_map/psum | solution.py:57
  167.3 1.0 constant_dynamic-slice_fusion.1
  168.3 0.2 copy.14
  168.5 1.3 fusion.12
  169.8 0.9 copy.16
  170.8 0.1 fusion.16
  170.8 97.1 %psum.15 = f32[256]{0:T(256)S(1)} all-reduce(f32[256]{0:T(256)S(1)} %fusion.16), channel_id=1, replica_groups=mesh['occ'=64,'aux'=8] {'occ','aux'}, use_global_device_ids=true, to_apply=%region_3.4 | all-reduce | flops 256 | bytes 2048 | tf_op jit(solution)/shard_map/psum | solution.py:75
  267.9 0.6 dynamic_slice.19
  (11 shorter events, 0.0 us)
Async XLA Ops:
  7.2 57.8 %copy-start = (f32[16,200]{1,0:T(8,128)S(1)}, f32[16,200]{1,0:T(8,128)}, u32[]{:S(2)}) copy-start(f32[16,200]{1,0:T(8,128)} %param.8) | copy-start | bytes 38404
  7.2 14.9 %copy-start.2 = (bf16[4,256,1024]{2,1,0:T(8,128)(2,1)S(1)}, bf16[4,256,1024]{2,1,0:T(8,128)(2,1)}, u32[]{:S(2)}) copy-start(bf16[4,256,1024]{2,1,0:T(8,128)(2,1)} %param.6) | copy-start | bytes 6291460
  7.2 160.1 %all-reduce.2.cloned.1.call-start = ((), (), s32[]{:S(2)}) async-start(), calls=%async_computation | async-start | bytes 6553600 | tf_op jit(solution)/shard_map/psum | solution.py:57
  7.2 28.0 %collective-permute-start = (bf16[4,256,1024]{2,1,0:T(8,128)(2,1)}, bf16[4,256,1024]{2,1,0:T(8,128)(2,1)}, u32[]{:S(2)}, u32[]{:S(2)}) collective-permute-start(bf16[4,256,1024]{2,1,0:T(8,128)(2,1)} %param.6), channel_id=1, source_target_pairs={{0,8},{8,16},{16,24},{24,32},{32,40},{40,48},{48,56},{56,64},{64,7... | collective-permute-start | bytes 6291464 | tf_op jit(solution)/shard_map/ppermute | solution.py:15
  12.0 27.7 %collective-permute-start.1 = (bf16[4,256,1024]{2,1,0:T(8,128)(2,1)}, bf16[4,256,1024]{2,1,0:T(8,128)(2,1)}, u32[]{:S(2)}, u32[]{:S(2)}) collective-permute-start(bf16[4,256,1024]{2,1,0:T(8,128)(2,1)} %param.6), channel_id=1, source_target_pairs={{8,0},{16,8},{24,16},{32,24},{40,32},{48,40},{56,48},{64,56},{72,6... | collective-permute-start | bytes 6291464 | tf_op jit(solution)/shard_map/ppermute | solution.py:17
  22.0 4.7 %copy-start.3 = (bf16[16,256,200]{1,2,0:T(8,128)(2,1)}, bf16[16,256,200]{1,2,0:T(8,128)(2,1)S(1)}, u32[]{:S(2)}) copy-start(bf16[16,256,200]{1,2,0:T(8,128)(2,1)S(1)} %broadcast_multiply_fusion) | copy-start | bytes 4915204
  45.1 7.7 %copy-start.4 = (bf16[16,256,200]{1,2,0:T(8,128)(2,1)S(1)}, bf16[16,256,200]{1,2,0:T(8,128)(2,1)}, u32[]{:S(2)}) copy-start(bf16[16,256,200]{1,2,0:T(8,128)(2,1)} %copy-done.3) | copy-start | bytes 4915204
  52.8 10.8 %copy-start.5 = (s32[16]{0:T(128)S(1)}, s32[16]{0:T(128)}, u32[]{:S(2)}) copy-start(s32[16]{0:T(128)} %param.10) | copy-start | bytes 196
  52.8 10.9 %copy-start.1 = (f32[256]{0:T(256)S(1)}, f32[256]{0:T(256)}, u32[]{:S(2)}) copy-start(f32[256]{0:T(256)} %param.9) | copy-start | bytes 3076
Sparse Core Ops, SparseCore 0:
  63.7 103.5 all-reduce.1
where the time goes:
time: 276 us; the launch traced here: 275 us
  waiting for transfers between devices  115 us (42%)
  blocking collectives  97.1 us (35%)
  matrix products  15.4 us (6%)
  between operations  14.1 us (5%)
  local copies, waits for them, and re-layouts  11.7 us (4%)
  starting transfers between devices  11.5 us (4%)
  other arithmetic  10.3 us (4%)
    psum x1, waiting for transfers between devices, shards(): totals = lax.psum(partials, 'aux')  102 us
    psum x1, blocking collectives, shards(): whole_sum = lax.psum(spread, ('occ', 'aux'))  97.1 us
    dot_general x1, matrix products, shards(): jnp.einsum('spk,sqk->spq', projected_own, projected_partner, preferred_el...  10.8 us
    ppermute x1, waiting for transfers between devices, padded(): lax.ppermute(tail, axis, [(i, (i + 1) % count) for i in range(ends)])  8.47 us
    gather x1, local copies, waits for them, and re-layouts, shards(): partner_blocks = jnp.take(nearby, window_slot, axis=0)  7.67 us
    ppermute x1, starting transfers between devices, padded(): lax.ppermute(head, axis, [((i + 1) % count, i) for i in range(ends)])  6.75 us
  transfers between devices with their start and end apart: 3, of which 3 were waited for; matrix products, arithmetic and copies ran while one was open for 3% of the time, Pallas kernels for 0%

commit v1 on v0

--- a/solution.py
+++ b/solution.py
@@ -2,6 +2,11 @@
 import jax.numpy as jnp
 from jax import lax
 from jax.sharding import PartitionSpec as P
+
+
+def gather_and_add(array, mesh_axis):
+    pieces = lax.all_gather(array, mesh_axis)
+    return jnp.sum(pieces, axis=0)
 
 
 def padded(cells, sides, width):
@@ -54,7 +59,7 @@
     )
     share_rows = pair_dev // lax.axis_size("aux")
     first_row = aux_place * share_rows
-    totals = lax.psum(partials, "aux")
+    totals = gather_and_add(partials, "aux")
     exchange_ints = lax.dynamic_slice_in_dim(totals, first_row, share_rows, 0)
     own_orbital = occ_place * orb_dev + jnp.arange(pair_dev, dtype=jnp.int32) // per_orbital
     mine_owner = lax.dynamic_slice_in_dim(own_orbital, first_row, share_rows, 0)

time: 276 us -> 454 us (1.64)
  waiting for transfers between devices: 115 us -> 279 us
  other arithmetic: 10.3 us -> 21.7 us
    all_gather x0 -> x1, waiting for transfers between devices: none -> 265 us  [gather_and_add(): pieces = lax.all_gather(array, mesh_axis)]
    psum x1 -> x0, waiting for transfers between devices: 102 us -> none  [shards(): totals = lax.psum(partials, 'aux')]
    reduce_sum x0 -> x1, other arithmetic: none -> 10.6 us  [gather_and_add(): return jnp.sum(pieces, axis=0)]
  transfers between devices with their start and end apart: 3 -> 3, of which waited for: 3 -> 3; matrix products, arithmetic and copies ran while one was open for 3% -> 2% of each run, Pallas kernels for 0% -> 0%
where the time goes in v1:
time: 454 us
  waiting for transfers between devices  279 us (61%)
  blocking collectives  97.1 us (21%)
  other arithmetic  21.7 us (5%)
  matrix products  17 us (4%)
  local copies, waits for them, and re-layouts  14.1 us (3%)
  between operations  14.1 us (3%)
  starting transfers between devices  10.7 us (2%)
    all_gather x1, waiting for transfers between devices, gather_and_add(): pieces = lax.all_gather(array, mesh_axis)  265 us
    psum x1, blocking collectives, shards(): whole_sum = lax.psum(spread, ('occ', 'aux'))  97.1 us
    dot_general x1, matrix products, shards(): jnp.einsum('spk,sqk->spq', projected_own, projected_partner, preferred_el...  10.8 us
    reduce_sum x1, other arithmetic, gather_and_add(): return jnp.sum(pieces, axis=0)  10.6 us
  transfers between devices with their start and end apart: 3, of which 3 were waited for; matrix products, arithmetic and copies ran while one was open for 2% of the time, Pallas kernels for 0%

profile of v1, /device:TPU:1, one launch (start us, length us, event | category | flops | bytes accessed | tf_op | source)
XLA Modules:
  0.0 453.7 jit_solution(16637419878309475972)
XLA Ops:
  7.2 0.0 copy-start
  7.2 0.0 all-gather.3.cloned.1.call-start
  7.2 8.8 %collective-permute-start.1 = (bf16[4,256,1024]{2,1,0:T(8,128)(2,1)}, bf16[4,256,1024]{2,1,0:T(8,128)(2,1)}, u32[]{:S(2)}, u32[]{:S(2)}) collective-permute-start(bf16[4,256,1024]{2,1,0:T(8,128)(2,1)} %param.6), channel_id=1, source_target_pairs={{8,0},{16,8},{24,16},{32,24},{40,32},{48,40},{56,48},{64,56},{72,6... | collective-permute-start | bytes 6291464 | tf_op jit(solution)/shard_map/ppermute | solution.py:22
  16.0 1.9 collective-permute-start
  17.9 0.7 compare_and_fusion
  18.6 0.7 fusion.13
  19.3 0.0 copy-start.2
  19.3 2.1 broadcast_multiply_fusion
  21.4 6.3 %convolution_convert_fusion = bf16[4,4,200,1024]{3,2,1,0:T(8,128)(2,1)} fusion(bf16[4,4,256,200]{2,3,1,0:T(8,128)(2,1)S(1)} %bitcast.18, bf16[4,256,1024]{2,1,0:T(8,128)(2,1)} %param.6), kind=kOutput, calls=%fused_computation.8 | convolution fusion | flops 1680998400 | bytes 10289152 | tf_op jit(solution)/shard_map/ornp,onk->orpk/dot_general | solution.py:42
  27.7 8.2 %collective-permute-done.1 = bf16[4,256,1024]{2,1,0:T(8,128)(2,1)} collective-permute-done((bf16[4,256,1024]{2,1,0:T(8,128)(2,1)}, bf16[4,256,1024]{2,1,0:T(8,128)(2,1)}, u32[]{:S(2)}, u32[]{:S(2)}) %collective-permute-start.1) | collective-permute-done | bytes 2097184 | tf_op jit(solution)/shard_map/ppermute | solution.py:22
  35.8 5.3 %collective-permute-done = bf16[4,256,1024]{2,1,0:T(8,128)(2,1)} collective-permute-done((bf16[4,256,1024]{2,1,0:T(8,128)(2,1)}, bf16[4,256,1024]{2,1,0:T(8,128)(2,1)}, u32[]{:S(2)}, u32[]{:S(2)}) %collective-permute-start) | collective-permute-done | bytes 2097184 | tf_op jit(solution)/shard_map/ppermute | solution.py:20
  41.2 0.0 copy-done.2
  41.2 5.5 %pad_maximum_fusion = bf16[12,256,1024]{2,1,0:T(8,128)(2,1)} fusion(bf16[4,256,1024]{2,1,0:T(8,128)(2,1)} %collective-permute-done.1, bf16[4,256,1024]{2,1,0:T(8,128)(2,1)S(1)} %copy-done.2, bf16[4,256,1024]{2,1,0:T(8,128)(2,1)} %collective-permute-done), kind=kLoop, calls=%fused_computation.7 | loop fusion | flops 6291456 | bytes 12582912 | tf_op jit(solution)/shard_map/concatenate | solution.py:18
  46.7 7.5 %gather_fusion = bf16[16,256,1024]{2,1,0:T(8,128)(2,1)} fusion(bf16[12,256,1024]{2,1,0:T(8,128)(2,1)} %pad_maximum_fusion, s32[1024]{0:T(1024)S(1)} %pad_clamp_fusion.2), kind=kCustom, calls=%fused_computation | custom fusion | bytes 16777280 | tf_op jit(solution)/shard_map/jit(_take)/gather | solution.py:53
  54.2 0.0 copy-start.3
  54.2 10.8 %fusion.9 = f32[16,200,200]{2,1,0:T(8,128)} fusion(bf16[16,200,1024]{2,1,0:T(8,128)(2,1)} %bitcast.19, bf16[16,256,200]{1,2,0:T(8,128)(2,1)S(1)} %broadcast_multiply_fusion, bf16[16,256,1024]{2,1,0:T(8,128)(2,1)} %gather_fusion, pred[16]{0:T(512)(128)(4,1)S(1)} %get-tuple-element.10), kind=kOutput, calls=%fused_computation.11 | convolution fusion | flops 2995912704 | bytes 19140624 | tf_op jit(solution)/shard_map/spk,sqk->spq/dot_general | solution.py:57
  65.0 0.0 all-gather.3.cloned.1.call-update
  65.0 0.0 copy-done.3
  65.0 0.1 compare_select_fusion
  65.1 0.0 copy-done.1
  65.1 0.6 gather_fusion.1
  65.8 0.6 gather_fusion.2
  66.4 0.0 copy-done
  66.4 265.5 %all-gather.3.cloned.1.call-done = f32[128,200,200]{2,1,0:T(8,128)} async-done(((f32[16,200,200]{2,1,0:T(8,128)}), f32[128,200,200]{2,1,0:T(8,128)}) %all-gather.3.cloned.1.call-update) | async-done | bytes 20480016 | tf_op jit(solution)/shard_map/all_gather | solution.py:8
  331.9 10.6 %reduce_sum.27 = f32[16,200,200]{2,1,0:T(8,128)S(1)} reduce(f32[8,16,200,200]{3,2,1,0:T(8,128)} %bitcast.17, f32[]{:T(128)} %constant.50.clone.1), dimensions={0}, to_apply=%region_0.1 | reduce | flops 4480000 | bytes 23040004 | tf_op jit(solution)/shard_map/reduce_sum | solution.py:9
  342.5 0.8 constant_dynamic-slice_fusion.1
  343.3 1.9 copy.15
  345.2 1.9 fusion.12
  347.2 1.9 copy.17
  349.1 0.1 fusion.16
  349.2 97.1 %psum.7 = f32[256]{0:T(256)S(1)} all-reduce(f32[256]{0:T(256)S(1)} %fusion.16), channel_id=1, replica_groups=mesh['occ'=64,'aux'=8] {'occ','aux'}, use_global_device_ids=true, to_apply=%region_3.4 | all-reduce | flops 256 | bytes 2048 | tf_op jit(solution)/shard_map/psum | solution.py:80
  446.3 0.6 dynamic_slice.19
  (8 shorter events, 0.0 us)
Async XLA Ops:
  7.2 59.3 %copy-start = (f32[16,200]{1,0:T(8,128)S(1)}, f32[16,200]{1,0:T(8,128)}, u32[]{:S(2)}) copy-start(f32[16,200]{1,0:T(8,128)} %param.8) | copy-start | bytes 38404
  7.2 324.7 %all-gather.3.cloned.1.call-start = ((), (), s32[]{:S(2)}) async-start(), calls=%async_computation | async-start | bytes 29491200 | tf_op jit(solution)/shard_map/all_gather | solution.py:8
  7.2 28.6 %collective-permute-start.1 = (bf16[4,256,1024]{2,1,0:T(8,128)(2,1)}, bf16[4,256,1024]{2,1,0:T(8,128)(2,1)}, u32[]{:S(2)}, u32[]{:S(2)}) collective-permute-start(bf16[4,256,1024]{2,1,0:T(8,128)(2,1)} %param.6), channel_id=1, source_target_pairs={{8,0},{16,8},{24,16},{32,24},{40,32},{48,40},{56,48},{64,56},{72,6... | collective-permute-start | bytes 6291464 | tf_op jit(solution)/shard_map/ppermute | solution.py:22
  16.0 25.2 %collective-permute-start = (bf16[4,256,1024]{2,1,0:T(8,128)(2,1)}, bf16[4,256,1024]{2,1,0:T(8,128)(2,1)}, u32[]{:S(2)}, u32[]{:S(2)}) collective-permute-start(bf16[4,256,1024]{2,1,0:T(8,128)(2,1)} %param.6), channel_id=1, source_target_pairs={{0,8},{8,16},{16,24},{24,32},{32,40},{40,48},{48,56},{56,64},{64,7... | collective-permute-start | bytes 6291464 | tf_op jit(solution)/shard_map/ppermute | solution.py:20
  19.3 21.9 %copy-start.2 = (bf16[4,256,1024]{2,1,0:T(8,128)(2,1)S(1)}, bf16[4,256,1024]{2,1,0:T(8,128)(2,1)}, u32[]{:S(2)}) copy-start(bf16[4,256,1024]{2,1,0:T(8,128)(2,1)} %param.6) | copy-start | bytes 6291460
  54.2 10.8 %copy-start.3 = (s32[16]{0:T(128)S(1)}, s32[16]{0:T(128)}, u32[]{:S(2)}) copy-start(s32[16]{0:T(128)} %param.10) | copy-start | bytes 196
  54.2 10.9 %copy-start.1 = (f32[256]{0:T(256)S(1)}, f32[256]{0:T(256)}, u32[]{:S(2)}) copy-start(f32[256]{0:T(256)} %param.9) | copy-start | bytes 3076
Sparse Core Ops, SparseCore 0:
  65.1 266.7 all-gather.2
